TPU v7x, 256 devices: a whole 4x4x8 slice. The times are simulated.
256 devices in a mesh: seq: 32 (over z, y), mp: 8 (over x, core).
Axes of the slice: x: 4, y: 4, z: 8, core: 2. Of those that a mesh axis runs over, the one named last changes fastest.
Arguments:
- scored_token_targets: int32 [8192], P('seq'), may hold values from 0 to 15999
- valid: int32 [8192], P('seq'), may hold values 0 or 1
- lengths: int32 [48], replicated, may hold values from 1 to 1024, 8192 in all
- owners: int32 [48], replicated, may hold values from 0 to 31
- holders: int32 [48], replicated, may hold values from -1 to 31, as said below
- mixer_input_x: bfloat16 [2, 8192, 3584], P(None, 'seq', 'mp'), may hold values from -6 to 6
- mixer_gate_input: bfloat16 [2, 8192, 3584], P(None, 'seq', 'mp'), may hold values from -6 to 6
- input_projection_b: bfloat16 [2, 8192, 64], P(None, 'seq'), may hold values from -2.390625 to 2.390625
- output_projection_c: bfloat16 [2, 8192, 64], P(None, 'seq'), may hold values from -2.390625 to 2.390625
- token_step_sizes: float32 [2, 8192, 56], P(None, 'seq', 'mp'), may hold values from 0.01 to 0.3
- head_decay_rate: float32 [2, 56], P(None, 'mp'), may hold values from 0.0002 to 1
- head_skip_scale: float32 [2, 56], P(None, 'mp'), may hold values from 0.5 to 1.5
- prompt_held_states: bfloat16 [2, 32, 56, 64, 64], P(None, 'seq', 'mp'), may hold values from -6 to 6
- shared_output_weight: bfloat16 [3584, 3584], P('mp'), may hold values from -0.09375 to 0.09375
- adapter_down_weight: bfloat16 [3584, 128], P('mp'), may hold values from -0.09375 to 0.09375
- adapter_up_weight: bfloat16 [128, 3584], replicated, may hold values from -0.5 to 0.5
- residual: bfloat16 [8192, 2, 3584], P('seq'), may hold values from -16 to 16
- final_norm_scale: float32 [3584], replicated, may hold values from 0.5 to 1.5
- vocab_head_weight: bfloat16 [3584, 16000], P('seq', 'mp'), may hold values from -8 to 8
Outputs:
- owner_sums: float32 [32, 48], P('seq')
- token_delta: float32 [8192], P('seq')
Inputs may be any that keep to these rules, and one draw needn't show every extreme that they name: `holders`: exactly 24 rollouts continue a prompt state; the others start from zeros.
All inputs are finite; a program needn't handle non-finite values. No bound on the sum of `valid` on one device may be relied on, other than what follows from the above.
Results may differ from a plain program's by a relative error of at most 0.035.
Values may be sent and summed in bfloat16 or wider, within the bound.
A program may use at most 128 MiB of HBM per device.

v0:
```python
import jax
import jax.numpy as jnp
from jax import lax
from jax.sharding import PartitionSpec as P

highest = lax.Precision.HIGHEST


def shifted(x, axis, by):
    count = lax.axis_size(axis)
    pairs = [(i, i + by) for i in range(count) if 0 <= i + by < count]
    return lax.ppermute(x, axis, pairs)


def root_norm(hidden, final_norm_scale):
    mean_sq = jnp.mean(hidden * hidden, axis=-1, keepdims=True)
    return (hidden * lax.rsqrt(mean_sq + 1e-05) * final_norm_scale).astype(jnp.bfloat16)


def shards(
    scored_token_targets,
    valid,
    lengths,
    owners,
    holders,
    mixer_input_x,
    mixer_gate_input,
    input_projection_b,
    output_projection_c,
    token_step_sizes,
    head_decay_rate,
    head_skip_scale,
    prompt_held_states,
    shared_output_weight,
    adapter_down_weight,
    adapter_up_weight,
    residual,
    final_norm_scale,
    vocab_head_weight,
):
    seq_count = lax.axis_size("seq")
    mp_count = lax.axis_size("mp")
    tok_rows = scored_token_targets.shape[0]
    models = mixer_input_x.shape[0]
    inner_local = mixer_input_x.shape[2]
    head_count = token_step_sizes.shape[2]
    head_dim = inner_local // head_count
    state_dim = input_projection_b.shape[2]
    roll_count = lengths.shape[0]
    first_row = lax.axis_index("seq") * tok_rows
    offsets = jnp.arange(tok_rows, dtype=jnp.int32)
    position = first_row + offsets
    starts = jnp.cumsum(lengths) - lengths
    rollout = jnp.sum((starts[None, :] <= position[:, None]).astype(jnp.int32), axis=1) - 1
    member_table = rollout[:, None] == jnp.arange(roll_count, dtype=jnp.int32)[None, :]
    start_local = jnp.sum(jnp.where(member_table, starts[None, :], 0), axis=1) - first_row
    holder_tok = jnp.sum(jnp.where(member_table, holders[None, :], 0), axis=1)
    borrowed = (start_local >= 0) & (holder_tok >= 0)
    prompt_pick = (
        (holder_tok[:, None] == jnp.arange(seq_count, dtype=jnp.int32)[None, :]) & borrowed[:, None]
    ).astype(jnp.float32)
    neg_rates = -head_decay_rate
    log_decay = jnp.cumsum(token_step_sizes * neg_rates[:, None, :], axis=1)
    before = jnp.take(log_decay, jnp.maximum(start_local - 1, 0), axis=1)
    before = jnp.where((start_local >= 1)[None, :, None], before, 0.0)
    x_values = mixer_input_x.astype(jnp.float32).reshape(models, tok_rows, head_count, head_dim)
    b_values = input_projection_b.astype(jnp.float32)
    c_values = output_projection_c.astype(jnp.float32)
    gram_matrix = jnp.einsum(
        "mtn,msn->mts", output_projection_c, input_projection_b, preferred_element_type=jnp.float32
    )
    causal = (rollout[:, None] == rollout[None, :]) & (offsets[None, :] <= offsets[:, None])
    log_gap = log_decay[:, :, None, :] - log_decay[:, None, :, :]
    mixing = jnp.where(
        causal[None, :, :, None], jnp.exp(jnp.where(causal[None, :, :, None], log_gap, 0.0)), 0.0
    )
    mixing = mixing * gram_matrix[..., None] * token_step_sizes[:, None, :, :]
    intra_out = jnp.einsum("mtsh,mshp->mthp", mixing, x_values, precision=highest)
    last_pick = prompt_pick[tok_rows - 1]
    zeros_state = jnp.zeros((models, head_count, head_dim, state_dim), jnp.float32)
    piece = lax.all_gather(prompt_held_states, "seq", axis=1, tiled=True)
    last_weight = last_pick.astype(jnp.bfloat16)
    picked = (prompt_pick[None, :, :, None] * c_values[:, :, None, :]).astype(jnp.bfloat16)
    projected = jnp.einsum("mtjn,mjhpn->mthp", picked, piece, preferred_element_type=jnp.float32)
    end_states = jnp.einsum("j,mjhpn->mhpn", last_weight, piece, preferred_element_type=jnp.float32)
    entry_decay = jnp.exp(log_decay - before)
    final_log = log_decay[:, tok_rows - 1, :]
    tail_mask = (rollout == rollout[tok_rows - 1]).astype(jnp.float32)
    end_weight = (
        jnp.exp(final_log[:, None, :] - log_decay) * token_step_sizes * tail_mask[None, :, None]
    )
    local_end = jnp.einsum("msh,mshp,msn->mhpn", end_weight, x_values, b_values, precision=highest)
    local_end = (
        local_end + jnp.exp(final_log - before[:, tok_rows - 1, :])[:, :, None, None] * end_states
    )
    carry_through = jnp.where(start_local[tok_rows - 1] < 0, jnp.exp(final_log), 0.0)

    def relay_step(step_index, incoming):
        outgoing = carry_through[:, :, None, None] * incoming + local_end
        return shifted(outgoing, "seq", 1)

    arriving = lax.fori_loop(0, seq_count - 1, relay_step, zeros_state)
    inherited = (start_local < 0).astype(jnp.float32)
    carried = jnp.einsum("mhpn,mtn->mthp", arriving, c_values, precision=highest)
    carried = carried * (jnp.exp(log_decay) * inherited[None, :, None])[..., None]
    output = (
        intra_out
        + carried
        + entry_decay[..., None] * projected
        + head_skip_scale[:, None, :, None] * x_values
    )
    output = output.reshape(models, tok_rows, inner_local)
    gated_output = (output * jax.nn.silu(mixer_gate_input.astype(jnp.float32))).astype(jnp.bfloat16)
    share_rows = tok_rows // mp_count
    base_output = jnp.einsum(
        "mti,id->tmd", gated_output, shared_output_weight, preferred_element_type=jnp.float32
    )
    low_rank_rows = jnp.dot(
        gated_output[0], adapter_down_weight, preferred_element_type=jnp.float32
    ).astype(jnp.bfloat16)
    adapter_output = jnp.dot(low_rank_rows, adapter_up_weight, preferred_element_type=jnp.float32)
    mixed = lax.psum_scatter(
        jnp.stack([base_output[:, 0] + adapter_output, base_output[:, 1]], axis=1).astype(
            jnp.bfloat16
        ),
        "mp",
        scatter_dimension=0,
        tiled=True,
    ).astype(jnp.float32)
    own_rows = lax.dynamic_slice_in_dim(residual, lax.axis_index("mp") * share_rows, share_rows, 0)
    normed_own = root_norm(own_rows.astype(jnp.float32) + mixed, final_norm_scale)
    normed = lax.all_gather(normed_own, "mp", axis=0, tiled=True)
    vocab_local = vocab_head_weight.shape[1]
    logits = jnp.einsum(
        "tmk,kv->mtv",
        normed,
        lax.all_gather(vocab_head_weight, "seq", axis=0, tiled=True),
        preferred_element_type=jnp.float32,
    )
    vocab_first = lax.axis_index("mp") * vocab_local
    target_hit = (
        scored_token_targets[:, None]
        == vocab_first + jnp.arange(vocab_local, dtype=jnp.int32)[None, :]
    )
    target_local = jnp.sum(jnp.where(target_hit[None], logits, 0.0), axis=2)
    local_max = jnp.max(logits, axis=2)
    vocab_top = lax.pmax(local_max, "mp")
    exp_sums = jnp.sum(jnp.exp(logits - vocab_top[..., None]), axis=2)
    vocab_total, target_logit = lax.psum((exp_sums, target_local), "mp")
    logprob = target_logit - vocab_top - jnp.log(vocab_total)
    token_delta = (logprob[0] - logprob[1]) * valid.astype(jnp.float32)
    roll_sums = jnp.dot(
        token_delta, member_table.astype(jnp.float32), precision=highest
    ) / lengths.astype(jnp.float32)
    owner_rows = (owners[None, :] == jnp.arange(seq_count, dtype=jnp.int32)[:, None]).astype(
        jnp.float32
    ) * roll_sums[None, :]
    owner_sums = lax.psum_scatter(owner_rows, "seq", scatter_dimension=0, tiled=True)
    return (owner_sums, token_delta)


def solution(mesh):
    placed = (
        P("seq"),
        P("seq"),
        P(),
        P(),
        P(),
        P(None, "seq", "mp"),
        P(None, "seq", "mp"),
        P(None, "seq", None),
        P(None, "seq", None),
        P(None, "seq", "mp"),
        P(None, "mp"),
        P(None, "mp"),
        P(None, "seq", "mp", None, None),
        P("mp", None),
        P("mp", None),
        P(),
        P("seq", None, None),
        P(),
        P("seq", "mp"),
    )
    return jax.shard_map(
        shards, mesh=mesh, in_specs=placed, out_specs=(P("seq", None), P("seq")), check_vma=False
    )
```

profile of v0, /device:TPU:0, one launch (start us, length us, event | category | flops | bytes accessed | tf_op | source)
XLA Modules:
  0.0 1076.7 jit_solution(12704770804620089405)
XLA Ops:
  35.8 69.4 %all-gather.4.cloned.1.call-done = bf16[2,32,7,64,64]{4,3,1,2,0:T(8,128)(2,1)} async-done(((bf16[2,1,7,64,64]{4,3,1,2,0:T(8,128)(2,1)}), bf16[2,32,7,64,64]{4,3,1,2,0:T(8,128)(2,1)}) %all-gather.4.cloned.1.call-update) | async-done | bytes 3670032 | tf_op jit(solution)/shard_map/all_gather | solution.py:81
  117.8 498.9 %while.10 = (s32[]{:T(128)}, f32[2,7,64,64]{3,2,1,0:T(8,128)}, f32[2,7]{1,0:T(2,128)S(1)}, f32[2,7,64,64]{3,2,1,0:T(8,128)}, s32[]{:T(128)}) while((s32[]{:T(128)}, f32[2,7,64,64]{3,2,1,0:T(8,128)}, f32[2,7]{1,0:T(2,128)S(1)}, f32[2,7,64,64]{3,2,1,0:T(8,128)}, s32[]{:T(128)}) %tuple.33), condition=%wide.region_7.8_spmd, body=%wide.region_6.7_spmd.sunk | while | flops 114690 | bytes 1605789 | solution.py:102
  122.8 8.9 collective-permute-done
  138.9 7.9 collective-permute-done
  230.1 7.5 collective-permute-start
  246.1 7.9 collective-permute-start
  254.0 7.5 collective-permute-done
  263.5 8.2 collective-permute-start
  271.7 8.6 collective-permute-done
  282.3 8.2 collective-permute-start
  290.5 9.8 collective-permute-done
  302.4 8.2 collective-permute-start
  310.6 9.9 collective-permute-done
  322.5 7.6 collective-permute-start
  330.1 8.7 collective-permute-done
  462.2 7.6 collective-permute-start
  479.0 8.2 collective-permute-start
  487.1 8.2 collective-permute-done
  497.4 8.2 collective-permute-start
  505.6 9.3 collective-permute-done
  517.0 8.2 collective-permute-start
  525.2 10.3 collective-permute-done
  537.5 7.6 collective-permute-start
  545.1 9.1 collective-permute-done
  563.4 8.0 collective-permute-done
  637.7 81.4 %reduce-scatter.2.cloned.1.call-done = bf16[32,2,3584]{2,0,1:T(8,128)(2,1)} async-done(((bf16[256,2,3584]{2,0,1:T(8,128)(2,1)}), bf16[32,2,3584]{2,0,1:T(8,128)(2,1)}) %reduce-scatter.2.cloned.1.call-update) | async-done | bytes 458768 | tf_op jit(solution)/shard_map/reduce_scatter | solution.py:122
  725.5 28.5 %all-gather.6.cloned.1.call-done = bf16[256,2,3584]{2,0,1:T(8,128)(2,1)} async-done(((bf16[32,2,3584]{2,0,1:T(8,128)(2,1)}), bf16[256,2,3584]{2,0,1:T(8,128)(2,1)}) %all-gather.6.cloned.1.call-update) | async-done | bytes 3670032 | tf_op jit(solution)/shard_map/all_gather | solution.py:132
  753.9 132.5 %all-gather.8.cloned.1.call-done = bf16[3584,2000]{1,0:T(8,128)(2,1)} async-done(((bf16[112,2000]{1,0:T(8,128)(2,1)}), bf16[3584,2000]{1,0:T(8,128)(2,1)}) %all-gather.8.cloned.1.call-update) | async-done | bytes 14336016 | tf_op jit(solution)/shard_map/all_gather | solution.py:137
  886.4 13.6 %fusion.6 = (f32[2,256]{1,0:T(2,128)S(1)}, f32[2,256]{1,0:T(2,128)S(1)}, f32[256,2,2000]{0,2,1:T(8,128)}) fusion(pred[256,2000]{0,1:T(8,128)(4,1)} %broadcast_compare_fusion, bf16[256,2,3584]{2,0,1:T(8,128)(2,1)} %all-gather.6.cloned.1.call-done, bf16[3584,2000]{1,0:T(8,128)(2,1)} %all-gather.8.cloned.1.call-done), kind=kOutput, calls=%fused_computation.14 | convolution fusion | flops 7343102976 | bytes 22618112 | tf_op jit(solution)/shard_map/tmk,kv->mtv/dot_general | solution.py:134
  900.0 14.3 %pmax.7 = f32[2,256]{1,0:T(2,128)S(1)} all-reduce(f32[2,256]{1,0:T(2,128)S(1)} %get-tuple-element.26), channel_id=1, replica_groups=mesh['seq'=32,'mp'=8] {'mp'}, use_global_device_ids=true, to_apply=%region_13.14 | all-reduce | flops 512 | bytes 4096 | tf_op jit(solution)/shard_map/pmax | solution.py:147
  917.1 12.4 %all-reduce.1 = (f32[2,256]{1,0:T(2,128)S(1)}, f32[2,256]{1,0:T(2,128)S(1)}) all-reduce(f32[2,256]{1,0:T(2,128)S(1)} %fusion.8, f32[2,256]{1,0:T(2,128)S(1)} %get-tuple-element.25), channel_id=1, replica_groups=mesh['seq'=32,'mp'=8] {'mp'}, use_global_device_ids=true, to_apply=%region_15.16 | all-reduce | flops 1024 | bytes 8192 | tf_op jit(solution)/shard_map/psum | solution.py:149
  929.7 139.3 %all-reduce = f32[32,48]{1,0:T(8,128)S(1)} all-reduce(f32[32,48]{1,0:T(8,128)S(1)} %fusion.54), channel_id=3, replica_groups=mesh['seq'=32,'mp'=8] {'seq'}, use_global_device_ids=true, to_apply=%region_16.17.clone | all-reduce | flops 1536 | bytes 12288
  (189 shorter events, 377.2 us)
Async XLA Ops:
  7.2 98.0 %all-gather.4.cloned.1.call-start = ((), (), s32[]{:S(2)}) async-start(), calls=%async_computation.1 | async-start | bytes 7569408 | tf_op jit(solution)/shard_map/all_gather | solution.py:81
  7.9 711.2 %reduce-scatter.2.cloned.1.call-start = ((), (), s32[]{:S(2)}) async-start(), calls=%async_computation.2 | async-start | bytes 4128768 | tf_op jit(solution)/shard_map/reduce_scatter | solution.py:122
  119.9 11.8 %collective-permute-start = (f32[2,7,64,64]{3,2,1,0:T(8,128)}, f32[2,7,64,64]{3,2,1,0:T(8,128)}, u32[]{:S(2)}, u32[]{:S(2)}) collective-permute-start(f32[2,7,64,64]{3,2,1,0:T(8,128)} %multiply_add_fusion.2), channel_id=1, source_target_pairs={{0,8},{8,16},{16,24},{24,32},{32,40},{40,48},{48,56},{56,64},{64,7... | collective-permute-start | bytes 688136 | tf_op jit(solution)/shard_map/while/body/eval_jaxpr/ppermute | solution.py:12
  133.7 13.1 %collective-permute-start = (f32[2,7,64,64]{3,2,1,0:T(8,128)}, f32[2,7,64,64]{3,2,1,0:T(8,128)}, u32[]{:S(2)}, u32[]{:S(2)}) collective-permute-start(f32[2,7,64,64]{3,2,1,0:T(8,128)} %multiply_add_fusion.2), channel_id=1, source_target_pairs={{0,8},{8,16},{16,24},{24,32},{32,40},{40,48},{48,56},{56,64},{64,7... | collective-permute-start | bytes 688136 | tf_op jit(solution)/shard_map/while/body/eval_jaxpr/ppermute | solution.py:12
  148.9 12.2 %collective-permute-start = (f32[2,7,64,64]{3,2,1,0:T(8,128)}, f32[2,7,64,64]{3,2,1,0:T(8,128)}, u32[]{:S(2)}, u32[]{:S(2)}) collective-permute-start(f32[2,7,64,64]{3,2,1,0:T(8,128)} %multiply_add_fusion.2), channel_id=1, source_target_pairs={{0,8},{8,16},{16,24},{24,32},{32,40},{40,48},{48,56},{56,64},{64,7... | collective-permute-start | bytes 688136 | tf_op jit(solution)/shard_map/while/body/eval_jaxpr/ppermute | solution.py:12
  201.9 11.4 %collective-permute-start = (f32[2,7,64,64]{3,2,1,0:T(8,128)}, f32[2,7,64,64]{3,2,1,0:T(8,128)}, u32[]{:S(2)}, u32[]{:S(2)}) collective-permute-start(f32[2,7,64,64]{3,2,1,0:T(8,128)} %multiply_add_fusion.2), channel_id=1, source_target_pairs={{0,8},{8,16},{16,24},{24,32},{32,40},{40,48},{48,56},{56,64},{64,7... | collective-permute-start | bytes 688136 | tf_op jit(solution)/shard_map/while/body/eval_jaxpr/ppermute | solution.py:12
  215.3 12.8 %collective-permute-start = (f32[2,7,64,64]{3,2,1,0:T(8,128)}, f32[2,7,64,64]{3,2,1,0:T(8,128)}, u32[]{:S(2)}, u32[]{:S(2)}) collective-permute-start(f32[2,7,64,64]{3,2,1,0:T(8,128)} %multiply_add_fusion.2), channel_id=1, source_target_pairs={{0,8},{8,16},{16,24},{24,32},{32,40},{40,48},{48,56},{56,64},{64,7... | collective-permute-start | bytes 688136 | tf_op jit(solution)/shard_map/while/body/eval_jaxpr/ppermute | solution.py:12
  230.1 13.9 %collective-permute-start = (f32[2,7,64,64]{3,2,1,0:T(8,128)}, f32[2,7,64,64]{3,2,1,0:T(8,128)}, u32[]{:S(2)}, u32[]{:S(2)}) collective-permute-start(f32[2,7,64,64]{3,2,1,0:T(8,128)} %multiply_add_fusion.2), channel_id=1, source_target_pairs={{0,8},{8,16},{16,24},{24,32},{32,40},{40,48},{48,56},{56,64},{64,7... | collective-permute-start | bytes 688136 | tf_op jit(solution)/shard_map/while/body/eval_jaxpr/ppermute | solution.py:12
  246.1 15.4 %collective-permute-start = (f32[2,7,64,64]{3,2,1,0:T(8,128)}, f32[2,7,64,64]{3,2,1,0:T(8,128)}, u32[]{:S(2)}, u32[]{:S(2)}) collective-permute-start(f32[2,7,64,64]{3,2,1,0:T(8,128)} %multiply_add_fusion.2), channel_id=1, source_target_pairs={{0,8},{8,16},{16,24},{24,32},{32,40},{40,48},{48,56},{56,64},{64,7... | collective-permute-start | bytes 688136 | tf_op jit(solution)/shard_map/while/body/eval_jaxpr/ppermute | solution.py:12
  263.5 16.8 %collective-permute-start = (f32[2,7,64,64]{3,2,1,0:T(8,128)}, f32[2,7,64,64]{3,2,1,0:T(8,128)}, u32[]{:S(2)}, u32[]{:S(2)}) collective-permute-start(f32[2,7,64,64]{3,2,1,0:T(8,128)} %multiply_add_fusion.2), channel_id=1, source_target_pairs={{0,8},{8,16},{16,24},{24,32},{32,40},{40,48},{48,56},{56,64},{64,7... | collective-permute-start | bytes 688136 | tf_op jit(solution)/shard_map/while/body/eval_jaxpr/ppermute | solution.py:12
  282.3 18.0 %collective-permute-start = (f32[2,7,64,64]{3,2,1,0:T(8,128)}, f32[2,7,64,64]{3,2,1,0:T(8,128)}, u32[]{:S(2)}, u32[]{:S(2)}) collective-permute-start(f32[2,7,64,64]{3,2,1,0:T(8,128)} %multiply_add_fusion.2), channel_id=1, source_target_pairs={{0,8},{8,16},{16,24},{24,32},{32,40},{40,48},{48,56},{56,64},{64,7... | collective-permute-start | bytes 688136 | tf_op jit(solution)/shard_map/while/body/eval_jaxpr/ppermute | solution.py:12
  302.4 18.1 %collective-permute-start = (f32[2,7,64,64]{3,2,1,0:T(8,128)}, f32[2,7,64,64]{3,2,1,0:T(8,128)}, u32[]{:S(2)}, u32[]{:S(2)}) collective-permute-start(f32[2,7,64,64]{3,2,1,0:T(8,128)} %multiply_add_fusion.2), channel_id=1, source_target_pairs={{0,8},{8,16},{16,24},{24,32},{32,40},{40,48},{48,56},{56,64},{64,7... | collective-permute-start | bytes 688136 | tf_op jit(solution)/shard_map/while/body/eval_jaxpr/ppermute | solution.py:12
  322.5 16.2 %collective-permute-start = (f32[2,7,64,64]{3,2,1,0:T(8,128)}, f32[2,7,64,64]{3,2,1,0:T(8,128)}, u32[]{:S(2)}, u32[]{:S(2)}) collective-permute-start(f32[2,7,64,64]{3,2,1,0:T(8,128)} %multiply_add_fusion.2), channel_id=1, source_target_pairs={{0,8},{8,16},{16,24},{24,32},{32,40},{40,48},{48,56},{56,64},{64,7... | collective-permute-start | bytes 688136 | tf_op jit(solution)/shard_map/while/body/eval_jaxpr/ppermute | solution.py:12
  340.8 13.8 %collective-permute-start = (f32[2,7,64,64]{3,2,1,0:T(8,128)}, f32[2,7,64,64]{3,2,1,0:T(8,128)}, u32[]{:S(2)}, u32[]{:S(2)}) collective-permute-start(f32[2,7,64,64]{3,2,1,0:T(8,128)} %multiply_add_fusion.2), channel_id=1, source_target_pairs={{0,8},{8,16},{16,24},{24,32},{32,40},{40,48},{48,56},{56,64},{64,7... | collective-permute-start | bytes 688136 | tf_op jit(solution)/shard_map/while/body/eval_jaxpr/ppermute | solution.py:12
  356.7 13.8 %collective-permute-start = (f32[2,7,64,64]{3,2,1,0:T(8,128)}, f32[2,7,64,64]{3,2,1,0:T(8,128)}, u32[]{:S(2)}, u32[]{:S(2)}) collective-permute-start(f32[2,7,64,64]{3,2,1,0:T(8,128)} %multiply_add_fusion.2), channel_id=1, source_target_pairs={{0,8},{8,16},{16,24},{24,32},{32,40},{40,48},{48,56},{56,64},{64,7... | collective-permute-start | bytes 688136 | tf_op jit(solution)/shard_map/while/body/eval_jaxpr/ppermute | solution.py:12
  372.5 12.9 %collective-permute-start = (f32[2,7,64,64]{3,2,1,0:T(8,128)}, f32[2,7,64,64]{3,2,1,0:T(8,128)}, u32[]{:S(2)}, u32[]{:S(2)}) collective-permute-start(f32[2,7,64,64]{3,2,1,0:T(8,128)} %multiply_add_fusion.2), channel_id=1, source_target_pairs={{0,8},{8,16},{16,24},{24,32},{32,40},{40,48},{48,56},{56,64},{64,7... | collective-permute-start | bytes 688136 | tf_op jit(solution)/shard_map/while/body/eval_jaxpr/ppermute | solution.py:12
  387.4 12.8 %collective-permute-start = (f32[2,7,64,64]{3,2,1,0:T(8,128)}, f32[2,7,64,64]{3,2,1,0:T(8,128)}, u32[]{:S(2)}, u32[]{:S(2)}) collective-permute-start(f32[2,7,64,64]{3,2,1,0:T(8,128)} %multiply_add_fusion.2), channel_id=1, source_target_pairs={{0,8},{8,16},{16,24},{24,32},{32,40},{40,48},{48,56},{56,64},{64,7... | collective-permute-start | bytes 688136 | tf_op jit(solution)/shard_map/while/body/eval_jaxpr/ppermute | solution.py:12
  402.3 12.8 %collective-permute-start = (f32[2,7,64,64]{3,2,1,0:T(8,128)}, f32[2,7,64,64]{3,2,1,0:T(8,128)}, u32[]{:S(2)}, u32[]{:S(2)}) collective-permute-start(f32[2,7,64,64]{3,2,1,0:T(8,128)} %multiply_add_fusion.2), channel_id=1, source_target_pairs={{0,8},{8,16},{16,24},{24,32},{32,40},{40,48},{48,56},{56,64},{64,7... | collective-permute-start | bytes 688136 | tf_op jit(solution)/shard_map/while/body/eval_jaxpr/ppermute | solution.py:12
  417.1 12.8 %collective-permute-start = (f32[2,7,64,64]{3,2,1,0:T(8,128)}, f32[2,7,64,64]{3,2,1,0:T(8,128)}, u32[]{:S(2)}, u32[]{:S(2)}) collective-permute-start(f32[2,7,64,64]{3,2,1,0:T(8,128)} %multiply_add_fusion.2), channel_id=1, source_target_pairs={{0,8},{8,16},{16,24},{24,32},{32,40},{40,48},{48,56},{56,64},{64,7... | collective-permute-start | bytes 688136 | tf_op jit(solution)/shard_map/while/body/eval_jaxpr/ppermute | solution.py:12
  431.9 12.8 %collective-permute-start = (f32[2,7,64,64]{3,2,1,0:T(8,128)}, f32[2,7,64,64]{3,2,1,0:T(8,128)}, u32[]{:S(2)}, u32[]{:S(2)}) collective-permute-start(f32[2,7,64,64]{3,2,1,0:T(8,128)} %multiply_add_fusion.2), channel_id=1, source_target_pairs={{0,8},{8,16},{16,24},{24,32},{32,40},{40,48},{48,56},{56,64},{64,7... | collective-permute-start | bytes 688136 | tf_op jit(solution)/shard_map/while/body/eval_jaxpr/ppermute | solution.py:12
  446.8 13.4 %collective-permute-start = (f32[2,7,64,64]{3,2,1,0:T(8,128)}, f32[2,7,64,64]{3,2,1,0:T(8,128)}, u32[]{:S(2)}, u32[]{:S(2)}) collective-permute-start(f32[2,7,64,64]{3,2,1,0:T(8,128)} %multiply_add_fusion.2), channel_id=1, source_target_pairs={{0,8},{8,16},{16,24},{24,32},{32,40},{40,48},{48,56},{56,64},{64,7... | collective-permute-start | bytes 688136 | tf_op jit(solution)/shard_map/while/body/eval_jaxpr/ppermute | solution.py:12
  462.2 14.7 %collective-permute-start = (f32[2,7,64,64]{3,2,1,0:T(8,128)}, f32[2,7,64,64]{3,2,1,0:T(8,128)}, u32[]{:S(2)}, u32[]{:S(2)}) collective-permute-start(f32[2,7,64,64]{3,2,1,0:T(8,128)} %multiply_add_fusion.2), channel_id=1, source_target_pairs={{0,8},{8,16},{16,24},{24,32},{32,40},{40,48},{48,56},{56,64},{64,7... | collective-permute-start | bytes 688136 | tf_op jit(solution)/shard_map/while/body/eval_jaxpr/ppermute | solution.py:12
  479.0 16.4 %collective-permute-start = (f32[2,7,64,64]{3,2,1,0:T(8,128)}, f32[2,7,64,64]{3,2,1,0:T(8,128)}, u32[]{:S(2)}, u32[]{:S(2)}) collective-permute-start(f32[2,7,64,64]{3,2,1,0:T(8,128)} %multiply_add_fusion.2), channel_id=1, source_target_pairs={{0,8},{8,16},{16,24},{24,32},{32,40},{40,48},{48,56},{56,64},{64,7... | collective-permute-start | bytes 688136 | tf_op jit(solution)/shard_map/while/body/eval_jaxpr/ppermute | solution.py:12
  497.4 17.5 %collective-permute-start = (f32[2,7,64,64]{3,2,1,0:T(8,128)}, f32[2,7,64,64]{3,2,1,0:T(8,128)}, u32[]{:S(2)}, u32[]{:S(2)}) collective-permute-start(f32[2,7,64,64]{3,2,1,0:T(8,128)} %multiply_add_fusion.2), channel_id=1, source_target_pairs={{0,8},{8,16},{16,24},{24,32},{32,40},{40,48},{48,56},{56,64},{64,7... | collective-permute-start | bytes 688136 | tf_op jit(solution)/shard_map/while/body/eval_jaxpr/ppermute | solution.py:12
  517.0 18.5 %collective-permute-start = (f32[2,7,64,64]{3,2,1,0:T(8,128)}, f32[2,7,64,64]{3,2,1,0:T(8,128)}, u32[]{:S(2)}, u32[]{:S(2)}) collective-permute-start(f32[2,7,64,64]{3,2,1,0:T(8,128)} %multiply_add_fusion.2), channel_id=1, source_target_pairs={{0,8},{8,16},{16,24},{24,32},{32,40},{40,48},{48,56},{56,64},{64,7... | collective-permute-start | bytes 688136 | tf_op jit(solution)/shard_map/while/body/eval_jaxpr/ppermute | solution.py:12
  537.5 16.7 %collective-permute-start = (f32[2,7,64,64]{3,2,1,0:T(8,128)}, f32[2,7,64,64]{3,2,1,0:T(8,128)}, u32[]{:S(2)}, u32[]{:S(2)}) collective-permute-start(f32[2,7,64,64]{3,2,1,0:T(8,128)} %multiply_add_fusion.2), channel_id=1, source_target_pairs={{0,8},{8,16},{16,24},{24,32},{32,40},{40,48},{48,56},{56,64},{64,7... | collective-permute-start | bytes 688136 | tf_op jit(solution)/shard_map/while/body/eval_jaxpr/ppermute | solution.py:12
  556.3 15.0 %collective-permute-start = (f32[2,7,64,64]{3,2,1,0:T(8,128)}, f32[2,7,64,64]{3,2,1,0:T(8,128)}, u32[]{:S(2)}, u32[]{:S(2)}) collective-permute-start(f32[2,7,64,64]{3,2,1,0:T(8,128)} %multiply_add_fusion.2), channel_id=1, source_target_pairs={{0,8},{8,16},{16,24},{24,32},{32,40},{40,48},{48,56},{56,64},{64,7... | collective-permute-start | bytes 688136 | tf_op jit(solution)/shard_map/while/body/eval_jaxpr/ppermute | solution.py:12
  573.4 13.7 %collective-permute-start = (f32[2,7,64,64]{3,2,1,0:T(8,128)}, f32[2,7,64,64]{3,2,1,0:T(8,128)}, u32[]{:S(2)}, u32[]{:S(2)}) collective-permute-start(f32[2,7,64,64]{3,2,1,0:T(8,128)} %multiply_add_fusion.2), channel_id=1, source_target_pairs={{0,8},{8,16},{16,24},{24,32},{32,40},{40,48},{48,56},{56,64},{64,7... | collective-permute-start | bytes 688136 | tf_op jit(solution)/shard_map/while/body/eval_jaxpr/ppermute | solution.py:12
  589.1 12.8 %collective-permute-start = (f32[2,7,64,64]{3,2,1,0:T(8,128)}, f32[2,7,64,64]{3,2,1,0:T(8,128)}, u32[]{:S(2)}, u32[]{:S(2)}) collective-permute-start(f32[2,7,64,64]{3,2,1,0:T(8,128)} %multiply_add_fusion.2), channel_id=1, source_target_pairs={{0,8},{8,16},{16,24},{24,32},{32,40},{40,48},{48,56},{56,64},{64,7... | collective-permute-start | bytes 688136 | tf_op jit(solution)/shard_map/while/body/eval_jaxpr/ppermute | solution.py:12
  603.9 12.8 %collective-permute-start = (f32[2,7,64,64]{3,2,1,0:T(8,128)}, f32[2,7,64,64]{3,2,1,0:T(8,128)}, u32[]{:S(2)}, u32[]{:S(2)}) collective-permute-start(f32[2,7,64,64]{3,2,1,0:T(8,128)} %multiply_add_fusion.2), channel_id=1, source_target_pairs={{0,8},{8,16},{16,24},{24,32},{32,40},{40,48},{48,56},{56,64},{64,7... | collective-permute-start | bytes 688136 | tf_op jit(solution)/shard_map/while/body/eval_jaxpr/ppermute | solution.py:12
  635.5 118.4 %all-gather.6.cloned.1.call-start = ((), (), s32[]{:S(2)}) async-start(), calls=%async_computation.3 | async-start | bytes 4128768 | tf_op jit(solution)/shard_map/all_gather | solution.py:132
  722.6 163.8 %all-gather.8.cloned.1.call-start = ((), (), s32[]{:S(2)}) async-start(), calls=%async_computation.4 | async-start | bytes 15138816 | tf_op jit(solution)/shard_map/all_gather | solution.py:137
  (22 other events, 2255.1 us)
Sparse Core Ops, SparseCore 0:
  10.6 94.5 all-gather.3
  635.6 83.3 reduce-scatter.1
  722.7 31.2 all-gather.5
  756.4 129.9 all-gather.7
where the time goes:
time: 1080 us
  waiting for transfers between devices  533 us (49%)
  starting transfers between devices  215 us (20%)
  blocking collectives  166 us (15%)
  other arithmetic  88.2 us (8%)
  matrix products  41 us (4%)
  local copies, waits for them, and re-layouts  18.2 us (2%)
  between operations  14.6 us (1%)
    ppermute x31, waiting for transfers between devices, shifted(): return lax.ppermute(x, axis, pairs)  220 us
    ppermute x31, starting transfers between devices, shifted(): return lax.ppermute(x, axis, pairs)  215 us
    unnamed x1, blocking collectives  139 us
    all_gather x1, waiting for transfers between devices, shards(): lax.all_gather(vocab_head_weight, 'seq', axis=0, tiled=True)  132 us
    reduce_scatter x1, waiting for transfers between devices, shards(): lax.psum_scatter(jnp.stack([base_output[:, 0] + adapter_output, base_outp...  81.4 us
    all_gather x1, waiting for transfers between devices, shards(): piece = lax.all_gather(prompt_held_states, 'seq', axis=1, tiled=True)  69.4 us
    add x31, other arithmetic, relay_step(): outgoing = carry_through[:, :, None, None] * incoming + local_end  63.3 us
    all_gather x1, waiting for transfers between devices, shards(): normed = lax.all_gather(normed_own, 'mp', axis=0, tiled=True)  28.5 us
  transfers between devices with their start and end apart: 35, of which 35 were waited for; matrix products, arithmetic and copies ran while one was open for 3% of the time, Pallas kernels for 0%

commit v1 on v0

--- a/solution.py
+++ b/solution.py
@@ -129,7 +129,18 @@
     ).astype(jnp.float32)
     own_rows = lax.dynamic_slice_in_dim(residual, lax.axis_index("mp") * share_rows, share_rows, 0)
     normed_own = root_norm(own_rows.astype(jnp.float32) + mixed, final_norm_scale)
-    normed = lax.all_gather(normed_own, "mp", axis=0, tiled=True)
+    slots = lax.axis_size("mp")
+    so_far_all = [(kk, (kk + 1) % slots) for kk in range(slots)]
+    pile = [(kk, (kk - 1) % slots) for kk in range(slots)]
+    t1, y_new = ([normed_own], [normed_own])
+    for _ in range(slots // 2):
+        t1.append(lax.ppermute(t1[-1], "mp", so_far_all))
+    dd = 0
+    while dd < (slots - 1) // 2:
+        y_new.append(lax.ppermute(y_new[-1], "mp", pile))
+        dd = dd + 1
+    field_out = jnp.concatenate([*t1[::-1], *y_new[1:]], axis=0)
+    normed = jnp.roll(field_out, (lax.axis_index("mp") - slots // 2) * normed_own.shape[0], axis=0)
     vocab_local = vocab_head_weight.shape[1]
     logits = jnp.einsum(
         "tmk,kv->mtv",

time: 1080 us -> 1040 us (0.963)
  waiting for transfers between devices: 533 us -> 477 us
  local copies, waits for them, and re-layouts: 18.2 us -> 29 us
    all_gather x1, waiting for transfers between devices: 132 us -> 79.6 us  [shards(): lax.all_gather(vocab_head_weight, 'seq', axis=0, tiled=True)]
    all_gather x1 -> x0, waiting for transfers between devices: 28.5 us -> none  [shards(): normed = lax.all_gather(normed_own, 'mp', axis=0, tiled=True)]
    ppermute x0 -> x7, waiting for transfers between devices: none -> 25.3 us  [the longest x4 25.3 us: shards(): t1.append(lax.ppermute(t1[-1], 'mp', so_far_all))]
    unnamed x41 -> x56, local copies, waits for them, and re-layouts: 6.97 us -> 19.1 us
  transfers between devices with their start and end apart: 35 -> 41, of which waited for: 35 -> 38; matrix products, arithmetic and copies ran while one was open for 3% -> 4% of each run, Pallas kernels for 0% -> 0%
where the time goes in v1:
time: 1040 us
  waiting for transfers between devices  477 us (46%)
  starting transfers between devices  224 us (22%)
  blocking collectives  166 us (16%)
  other arithmetic  87.7 us (8%)
  matrix products  41.2 us (4%)
  local copies, waits for them, and re-layouts  29 us (3%)
  between operations  14.6 us (1%)
    ppermute x31, waiting for transfers between devices, shifted(): return lax.ppermute(x, axis, pairs)  220 us
    ppermute x31, starting transfers between devices, shifted(): return lax.ppermute(x, axis, pairs)  215 us
    unnamed x1, blocking collectives  139 us
    reduce_scatter x1, waiting for transfers between devices, shards(): lax.psum_scatter(jnp.stack([base_output[:, 0] + adapter_output, base_outp...  81.5 us
    all_gather x1, waiting for transfers between devices, shards(): lax.all_gather(vocab_head_weight, 'seq', axis=0, tiled=True)  79.6 us
    all_gather x1, waiting for transfers between devices, shards(): piece = lax.all_gather(prompt_held_states, 'seq', axis=1, tiled=True)  69.4 us
    add x31, other arithmetic, relay_step(): outgoing = carry_through[:, :, None, None] * incoming + local_end  63.3 us
    ppermute x4, waiting for transfers between devices, shards(): t1.append(lax.ppermute(t1[-1], 'mp', so_far_all))  25.3 us
  transfers between devices with their start and end apart: 41, of which 38 were waited for; matrix products, arithmetic and copies ran while one was open for 4% of the time, Pallas kernels for 0%

profile of v1, /device:TPU:0, one launch (start us, length us, event | category | flops | bytes accessed | tf_op | source)
XLA Modules:
  0.0 1040.1 jit_solution(14838279720373486931)
XLA Ops:
  35.8 69.4 %all-gather.3.cloned.1.call-done = bf16[2,32,7,64,64]{4,3,1,2,0:T(8,128)(2,1)} async-done(((bf16[2,1,7,64,64]{4,3,1,2,0:T(8,128)(2,1)}), bf16[2,32,7,64,64]{4,3,1,2,0:T(8,128)(2,1)}) %all-gather.3.cloned.1.call-update) | async-done | bytes 3670032 | tf_op jit(solution)/shard_map/all_gather | solution.py:81
  117.8 498.9 %while.10 = (s32[]{:T(128)}, f32[2,7,64,64]{3,2,1,0:T(8,128)}, f32[2,7]{1,0:T(2,128)S(1)}, f32[2,7,64,64]{3,2,1,0:T(8,128)}, s32[]{:T(128)}) while((s32[]{:T(128)}, f32[2,7,64,64]{3,2,1,0:T(8,128)}, f32[2,7]{1,0:T(2,128)S(1)}, f32[2,7,64,64]{3,2,1,0:T(8,128)}, s32[]{:T(128)}) %tuple.33), condition=%wide.region_7.8_spmd, body=%wide.region_6.7_spmd.sunk | while | flops 114690 | bytes 1605789 | solution.py:102
  122.8 8.9 collective-permute-done
  138.9 7.9 collective-permute-done
  230.1 7.5 collective-permute-start
  246.1 7.9 collective-permute-start
  254.0 7.5 collective-permute-done
  263.5 8.2 collective-permute-start
  271.7 8.6 collective-permute-done
  282.3 8.2 collective-permute-start
  290.5 9.8 collective-permute-done
  302.4 8.2 collective-permute-start
  310.6 9.9 collective-permute-done
  322.5 7.6 collective-permute-start
  330.1 8.7 collective-permute-done
  462.2 7.6 collective-permute-start
  479.0 8.2 collective-permute-start
  487.1 8.2 collective-permute-done
  497.4 8.2 collective-permute-start
  505.6 9.3 collective-permute-done
  517.0 8.2 collective-permute-start
  525.2 10.3 collective-permute-done
  537.5 7.6 collective-permute-start
  545.1 9.1 collective-permute-done
  563.4 8.0 collective-permute-done
  636.8 81.5 %reduce-scatter.2.cloned.1.call-done = bf16[32,2,3584]{2,0,1:T(8,128)(2,1)} async-done(((bf16[256,2,3584]{2,0,1:T(8,128)(2,1)}), bf16[32,2,3584]{2,0,1:T(8,128)(2,1)}) %reduce-scatter.2.cloned.1.call-update) | async-done | bytes 458768 | tf_op jit(solution)/shard_map/reduce_scatter | solution.py:122
  720.7 9.1 collective-permute-done.1
  770.1 79.6 %all-gather.5.cloned.1.call-done = bf16[3584,2000]{1,0:T(8,128)(2,1)} async-done(((bf16[112,2000]{1,0:T(8,128)(2,1)}), bf16[3584,2000]{1,0:T(8,128)(2,1)}) %all-gather.5.cloned.1.call-update) | async-done | bytes 14336016 | tf_op jit(solution)/shard_map/all_gather | solution.py:148
  849.7 13.8 %fusion.6 = (f32[2,256]{1,0:T(2,128)S(1)}, f32[2,256]{1,0:T(2,128)S(1)}, f32[256,2,2000]{0,2,1:T(8,128)}) fusion(pred[256,2000]{0,1:T(8,128)(4,1)} %broadcast_compare_fusion, bf16[3584,2000]{1,0:T(8,128)(2,1)} %all-gather.5.cloned.1.call-done, bf16[512,2,3584]{2,0,1:T(8,128)(2,1)} %constant_dynamic-update-slice_fusion, s32[]{:T(128)S(6)} %select_n.63), kind=kOutput, calls=%fused_computation.14 | convolution fusion | flops 7343102976 | bytes 22962180 | tf_op jit(solution)/shard_map/tmk,kv->mtv/dot_general | solution.py:145
  863.6 14.2 %pmax.7 = f32[2,256]{1,0:T(2,128)S(1)} all-reduce(f32[2,256]{1,0:T(2,128)S(1)} %get-tuple-element.26), channel_id=1, replica_groups=mesh['seq'=32,'mp'=8] {'mp'}, use_global_device_ids=true, to_apply=%region_13.14 | all-reduce | flops 512 | bytes 4096 | tf_op jit(solution)/shard_map/pmax | solution.py:158
  880.4 12.4 %all-reduce.1 = (f32[2,256]{1,0:T(2,128)S(1)}, f32[2,256]{1,0:T(2,128)S(1)}) all-reduce(f32[2,256]{1,0:T(2,128)S(1)} %fusion.8, f32[2,256]{1,0:T(2,128)S(1)} %get-tuple-element.25), channel_id=1, replica_groups=mesh['seq'=32,'mp'=8] {'mp'}, use_global_device_ids=true, to_apply=%region_15.16 | all-reduce | flops 1024 | bytes 8192 | tf_op jit(solution)/shard_map/psum | solution.py:160
  893.1 139.3 %all-reduce = f32[32,48]{1,0:T(8,128)S(1)} all-reduce(f32[32,48]{1,0:T(8,128)S(1)} %fusion.55), channel_id=3, replica_groups=mesh['seq'=32,'mp'=8] {'seq'}, use_global_device_ids=true, to_apply=%region_16.17.clone | all-reduce | flops 1536 | bytes 12288
  (216 shorter events, 412.7 us)
Async XLA Ops:
  7.2 98.0 %all-gather.3.cloned.1.call-start = ((), (), s32[]{:S(2)}) async-start(), calls=%async_computation.1 | async-start | bytes 7569408 | tf_op jit(solution)/shard_map/all_gather | solution.py:81
  7.9 710.4 %reduce-scatter.2.cloned.1.call-start = ((), (), s32[]{:S(2)}) async-start(), calls=%async_computation.2 | async-start | bytes 4128768 | tf_op jit(solution)/shard_map/reduce_scatter | solution.py:122
  119.9 11.8 %collective-permute-start = (f32[2,7,64,64]{3,2,1,0:T(8,128)}, f32[2,7,64,64]{3,2,1,0:T(8,128)}, u32[]{:S(2)}, u32[]{:S(2)}) collective-permute-start(f32[2,7,64,64]{3,2,1,0:T(8,128)} %multiply_add_fusion.2), channel_id=1, source_target_pairs={{0,8},{8,16},{16,24},{24,32},{32,40},{40,48},{48,56},{56,64},{64,7... | collective-permute-start | bytes 688136 | tf_op jit(solution)/shard_map/while/body/eval_jaxpr/ppermute | solution.py:12
  133.7 13.1 %collective-permute-start = (f32[2,7,64,64]{3,2,1,0:T(8,128)}, f32[2,7,64,64]{3,2,1,0:T(8,128)}, u32[]{:S(2)}, u32[]{:S(2)}) collective-permute-start(f32[2,7,64,64]{3,2,1,0:T(8,128)} %multiply_add_fusion.2), channel_id=1, source_target_pairs={{0,8},{8,16},{16,24},{24,32},{32,40},{40,48},{48,56},{56,64},{64,7... | collective-permute-start | bytes 688136 | tf_op jit(solution)/shard_map/while/body/eval_jaxpr/ppermute | solution.py:12
  148.9 12.2 %collective-permute-start = (f32[2,7,64,64]{3,2,1,0:T(8,128)}, f32[2,7,64,64]{3,2,1,0:T(8,128)}, u32[]{:S(2)}, u32[]{:S(2)}) collective-permute-start(f32[2,7,64,64]{3,2,1,0:T(8,128)} %multiply_add_fusion.2), channel_id=1, source_target_pairs={{0,8},{8,16},{16,24},{24,32},{32,40},{40,48},{48,56},{56,64},{64,7... | collective-permute-start | bytes 688136 | tf_op jit(solution)/shard_map/while/body/eval_jaxpr/ppermute | solution.py:12
  201.9 11.4 %collective-permute-start = (f32[2,7,64,64]{3,2,1,0:T(8,128)}, f32[2,7,64,64]{3,2,1,0:T(8,128)}, u32[]{:S(2)}, u32[]{:S(2)}) collective-permute-start(f32[2,7,64,64]{3,2,1,0:T(8,128)} %multiply_add_fusion.2), channel_id=1, source_target_pairs={{0,8},{8,16},{16,24},{24,32},{32,40},{40,48},{48,56},{56,64},{64,7... | collective-permute-start | bytes 688136 | tf_op jit(solution)/shard_map/while/body/eval_jaxpr/ppermute | solution.py:12
  215.3 12.8 %collective-permute-start = (f32[2,7,64,64]{3,2,1,0:T(8,128)}, f32[2,7,64,64]{3,2,1,0:T(8,128)}, u32[]{:S(2)}, u32[]{:S(2)}) collective-permute-start(f32[2,7,64,64]{3,2,1,0:T(8,128)} %multiply_add_fusion.2), channel_id=1, source_target_pairs={{0,8},{8,16},{16,24},{24,32},{32,40},{40,48},{48,56},{56,64},{64,7... | collective-permute-start | bytes 688136 | tf_op jit(solution)/shard_map/while/body/eval_jaxpr/ppermute | solution.py:12
  230.1 13.9 %collective-permute-start = (f32[2,7,64,64]{3,2,1,0:T(8,128)}, f32[2,7,64,64]{3,2,1,0:T(8,128)}, u32[]{:S(2)}, u32[]{:S(2)}) collective-permute-start(f32[2,7,64,64]{3,2,1,0:T(8,128)} %multiply_add_fusion.2), channel_id=1, source_target_pairs={{0,8},{8,16},{16,24},{24,32},{32,40},{40,48},{48,56},{56,64},{64,7... | collective-permute-start | bytes 688136 | tf_op jit(solution)/shard_map/while/body/eval_jaxpr/ppermute | solution.py:12
  246.1 15.4 %collective-permute-start = (f32[2,7,64,64]{3,2,1,0:T(8,128)}, f32[2,7,64,64]{3,2,1,0:T(8,128)}, u32[]{:S(2)}, u32[]{:S(2)}) collective-permute-start(f32[2,7,64,64]{3,2,1,0:T(8,128)} %multiply_add_fusion.2), channel_id=1, source_target_pairs={{0,8},{8,16},{16,24},{24,32},{32,40},{40,48},{48,56},{56,64},{64,7... | collective-permute-start | bytes 688136 | tf_op jit(solution)/shard_map/while/body/eval_jaxpr/ppermute | solution.py:12
  263.5 16.8 %collective-permute-start = (f32[2,7,64,64]{3,2,1,0:T(8,128)}, f32[2,7,64,64]{3,2,1,0:T(8,128)}, u32[]{:S(2)}, u32[]{:S(2)}) collective-permute-start(f32[2,7,64,64]{3,2,1,0:T(8,128)} %multiply_add_fusion.2), channel_id=1, source_target_pairs={{0,8},{8,16},{16,24},{24,32},{32,40},{40,48},{48,56},{56,64},{64,7... | collective-permute-start | bytes 688136 | tf_op jit(solution)/shard_map/while/body/eval_jaxpr/ppermute | solution.py:12
  282.3 18.0 %collective-permute-start = (f32[2,7,64,64]{3,2,1,0:T(8,128)}, f32[2,7,64,64]{3,2,1,0:T(8,128)}, u32[]{:S(2)}, u32[]{:S(2)}) collective-permute-start(f32[2,7,64,64]{3,2,1,0:T(8,128)} %multiply_add_fusion.2), channel_id=1, source_target_pairs={{0,8},{8,16},{16,24},{24,32},{32,40},{40,48},{48,56},{56,64},{64,7... | collective-permute-start | bytes 688136 | tf_op jit(solution)/shard_map/while/body/eval_jaxpr/ppermute | solution.py:12
  302.4 18.1 %collective-permute-start = (f32[2,7,64,64]{3,2,1,0:T(8,128)}, f32[2,7,64,64]{3,2,1,0:T(8,128)}, u32[]{:S(2)}, u32[]{:S(2)}) collective-permute-start(f32[2,7,64,64]{3,2,1,0:T(8,128)} %multiply_add_fusion.2), channel_id=1, source_target_pairs={{0,8},{8,16},{16,24},{24,32},{32,40},{40,48},{48,56},{56,64},{64,7... | collective-permute-start | bytes 688136 | tf_op jit(solution)/shard_map/while/body/eval_jaxpr/ppermute | solution.py:12
  322.5 16.2 %collective-permute-start = (f32[2,7,64,64]{3,2,1,0:T(8,128)}, f32[2,7,64,64]{3,2,1,0:T(8,128)}, u32[]{:S(2)}, u32[]{:S(2)}) collective-permute-start(f32[2,7,64,64]{3,2,1,0:T(8,128)} %multiply_add_fusion.2), channel_id=1, source_target_pairs={{0,8},{8,16},{16,24},{24,32},{32,40},{40,48},{48,56},{56,64},{64,7... | collective-permute-start | bytes 688136 | tf_op jit(solution)/shard_map/while/body/eval_jaxpr/ppermute | solution.py:12
  340.8 13.8 %collective-permute-start = (f32[2,7,64,64]{3,2,1,0:T(8,128)}, f32[2,7,64,64]{3,2,1,0:T(8,128)}, u32[]{:S(2)}, u32[]{:S(2)}) collective-permute-start(f32[2,7,64,64]{3,2,1,0:T(8,128)} %multiply_add_fusion.2), channel_id=1, source_target_pairs={{0,8},{8,16},{16,24},{24,32},{32,40},{40,48},{48,56},{56,64},{64,7... | collective-permute-start | bytes 688136 | tf_op jit(solution)/shard_map/while/body/eval_jaxpr/ppermute | solution.py:12
  356.7 13.8 %collective-permute-start = (f32[2,7,64,64]{3,2,1,0:T(8,128)}, f32[2,7,64,64]{3,2,1,0:T(8,128)}, u32[]{:S(2)}, u32[]{:S(2)}) collective-permute-start(f32[2,7,64,64]{3,2,1,0:T(8,128)} %multiply_add_fusion.2), channel_id=1, source_target_pairs={{0,8},{8,16},{16,24},{24,32},{32,40},{40,48},{48,56},{56,64},{64,7... | collective-permute-start | bytes 688136 | tf_op jit(solution)/shard_map/while/body/eval_jaxpr/ppermute | solution.py:12
  372.5 12.9 %collective-permute-start = (f32[2,7,64,64]{3,2,1,0:T(8,128)}, f32[2,7,64,64]{3,2,1,0:T(8,128)}, u32[]{:S(2)}, u32[]{:S(2)}) collective-permute-start(f32[2,7,64,64]{3,2,1,0:T(8,128)} %multiply_add_fusion.2), channel_id=1, source_target_pairs={{0,8},{8,16},{16,24},{24,32},{32,40},{40,48},{48,56},{56,64},{64,7... | collective-permute-start | bytes 688136 | tf_op jit(solution)/shard_map/while/body/eval_jaxpr/ppermute | solution.py:12
  387.4 12.8 %collective-permute-start = (f32[2,7,64,64]{3,2,1,0:T(8,128)}, f32[2,7,64,64]{3,2,1,0:T(8,128)}, u32[]{:S(2)}, u32[]{:S(2)}) collective-permute-start(f32[2,7,64,64]{3,2,1,0:T(8,128)} %multiply_add_fusion.2), channel_id=1, source_target_pairs={{0,8},{8,16},{16,24},{24,32},{32,40},{40,48},{48,56},{56,64},{64,7... | collective-permute-start | bytes 688136 | tf_op jit(solution)/shard_map/while/body/eval_jaxpr/ppermute | solution.py:12
  402.3 12.8 %collective-permute-start = (f32[2,7,64,64]{3,2,1,0:T(8,128)}, f32[2,7,64,64]{3,2,1,0:T(8,128)}, u32[]{:S(2)}, u32[]{:S(2)}) collective-permute-start(f32[2,7,64,64]{3,2,1,0:T(8,128)} %multiply_add_fusion.2), channel_id=1, source_target_pairs={{0,8},{8,16},{16,24},{24,32},{32,40},{40,48},{48,56},{56,64},{64,7... | collective-permute-start | bytes 688136 | tf_op jit(solution)/shard_map/while/body/eval_jaxpr/ppermute | solution.py:12
  417.1 12.8 %collective-permute-start = (f32[2,7,64,64]{3,2,1,0:T(8,128)}, f32[2,7,64,64]{3,2,1,0:T(8,128)}, u32[]{:S(2)}, u32[]{:S(2)}) collective-permute-start(f32[2,7,64,64]{3,2,1,0:T(8,128)} %multiply_add_fusion.2), channel_id=1, source_target_pairs={{0,8},{8,16},{16,24},{24,32},{32,40},{40,48},{48,56},{56,64},{64,7... | collective-permute-start | bytes 688136 | tf_op jit(solution)/shard_map/while/body/eval_jaxpr/ppermute | solution.py:12
  431.9 12.8 %collective-permute-start = (f32[2,7,64,64]{3,2,1,0:T(8,128)}, f32[2,7,64,64]{3,2,1,0:T(8,128)}, u32[]{:S(2)}, u32[]{:S(2)}) collective-permute-start(f32[2,7,64,64]{3,2,1,0:T(8,128)} %multiply_add_fusion.2), channel_id=1, source_target_pairs={{0,8},{8,16},{16,24},{24,32},{32,40},{40,48},{48,56},{56,64},{64,7... | collective-permute-start | bytes 688136 | tf_op jit(solution)/shard_map/while/body/eval_jaxpr/ppermute | solution.py:12
  446.8 13.4 %collective-permute-start = (f32[2,7,64,64]{3,2,1,0:T(8,128)}, f32[2,7,64,64]{3,2,1,0:T(8,128)}, u32[]{:S(2)}, u32[]{:S(2)}) collective-permute-start(f32[2,7,64,64]{3,2,1,0:T(8,128)} %multiply_add_fusion.2), channel_id=1, source_target_pairs={{0,8},{8,16},{16,24},{24,32},{32,40},{40,48},{48,56},{56,64},{64,7... | collective-permute-start | bytes 688136 | tf_op jit(solution)/shard_map/while/body/eval_jaxpr/ppermute | solution.py:12
  462.2 14.7 %collective-permute-start = (f32[2,7,64,64]{3,2,1,0:T(8,128)}, f32[2,7,64,64]{3,2,1,0:T(8,128)}, u32[]{:S(2)}, u32[]{:S(2)}) collective-permute-start(f32[2,7,64,64]{3,2,1,0:T(8,128)} %multiply_add_fusion.2), channel_id=1, source_target_pairs={{0,8},{8,16},{16,24},{24,32},{32,40},{40,48},{48,56},{56,64},{64,7... | collective-permute-start | bytes 688136 | tf_op jit(solution)/shard_map/while/body/eval_jaxpr/ppermute | solution.py:12
  479.0 16.4 %collective-permute-start = (f32[2,7,64,64]{3,2,1,0:T(8,128)}, f32[2,7,64,64]{3,2,1,0:T(8,128)}, u32[]{:S(2)}, u32[]{:S(2)}) collective-permute-start(f32[2,7,64,64]{3,2,1,0:T(8,128)} %multiply_add_fusion.2), channel_id=1, source_target_pairs={{0,8},{8,16},{16,24},{24,32},{32,40},{40,48},{48,56},{56,64},{64,7... | collective-permute-start | bytes 688136 | tf_op jit(solution)/shard_map/while/body/eval_jaxpr/ppermute | solution.py:12
  497.4 17.5 %collective-permute-start = (f32[2,7,64,64]{3,2,1,0:T(8,128)}, f32[2,7,64,64]{3,2,1,0:T(8,128)}, u32[]{:S(2)}, u32[]{:S(2)}) collective-permute-start(f32[2,7,64,64]{3,2,1,0:T(8,128)} %multiply_add_fusion.2), channel_id=1, source_target_pairs={{0,8},{8,16},{16,24},{24,32},{32,40},{40,48},{48,56},{56,64},{64,7... | collective-permute-start | bytes 688136 | tf_op jit(solution)/shard_map/while/body/eval_jaxpr/ppermute | solution.py:12
  517.0 18.5 %collective-permute-start = (f32[2,7,64,64]{3,2,1,0:T(8,128)}, f32[2,7,64,64]{3,2,1,0:T(8,128)}, u32[]{:S(2)}, u32[]{:S(2)}) collective-permute-start(f32[2,7,64,64]{3,2,1,0:T(8,128)} %multiply_add_fusion.2), channel_id=1, source_target_pairs={{0,8},{8,16},{16,24},{24,32},{32,40},{40,48},{48,56},{56,64},{64,7... | collective-permute-start | bytes 688136 | tf_op jit(solution)/shard_map/while/body/eval_jaxpr/ppermute | solution.py:12
  537.5 16.7 %collective-permute-start = (f32[2,7,64,64]{3,2,1,0:T(8,128)}, f32[2,7,64,64]{3,2,1,0:T(8,128)}, u32[]{:S(2)}, u32[]{:S(2)}) collective-permute-start(f32[2,7,64,64]{3,2,1,0:T(8,128)} %multiply_add_fusion.2), channel_id=1, source_target_pairs={{0,8},{8,16},{16,24},{24,32},{32,40},{40,48},{48,56},{56,64},{64,7... | collective-permute-start | bytes 688136 | tf_op jit(solution)/shard_map/while/body/eval_jaxpr/ppermute | solution.py:12
  556.3 15.0 %collective-permute-start = (f32[2,7,64,64]{3,2,1,0:T(8,128)}, f32[2,7,64,64]{3,2,1,0:T(8,128)}, u32[]{:S(2)}, u32[]{:S(2)}) collective-permute-start(f32[2,7,64,64]{3,2,1,0:T(8,128)} %multiply_add_fusion.2), channel_id=1, source_target_pairs={{0,8},{8,16},{16,24},{24,32},{32,40},{40,48},{48,56},{56,64},{64,7... | collective-permute-start | bytes 688136 | tf_op jit(solution)/shard_map/while/body/eval_jaxpr/ppermute | solution.py:12
  573.4 13.7 %collective-permute-start = (f32[2,7,64,64]{3,2,1,0:T(8,128)}, f32[2,7,64,64]{3,2,1,0:T(8,128)}, u32[]{:S(2)}, u32[]{:S(2)}) collective-permute-start(f32[2,7,64,64]{3,2,1,0:T(8,128)} %multiply_add_fusion.2), channel_id=1, source_target_pairs={{0,8},{8,16},{16,24},{24,32},{32,40},{40,48},{48,56},{56,64},{64,7... | collective-permute-start | bytes 688136 | tf_op jit(solution)/shard_map/while/body/eval_jaxpr/ppermute | solution.py:12
  589.1 12.8 %collective-permute-start = (f32[2,7,64,64]{3,2,1,0:T(8,128)}, f32[2,7,64,64]{3,2,1,0:T(8,128)}, u32[]{:S(2)}, u32[]{:S(2)}) collective-permute-start(f32[2,7,64,64]{3,2,1,0:T(8,128)} %multiply_add_fusion.2), channel_id=1, source_target_pairs={{0,8},{8,16},{16,24},{24,32},{32,40},{40,48},{48,56},{56,64},{64,7... | collective-permute-start | bytes 688136 | tf_op jit(solution)/shard_map/while/body/eval_jaxpr/ppermute | solution.py:12
  603.9 12.8 %collective-permute-start = (f32[2,7,64,64]{3,2,1,0:T(8,128)}, f32[2,7,64,64]{3,2,1,0:T(8,128)}, u32[]{:S(2)}, u32[]{:S(2)}) collective-permute-start(f32[2,7,64,64]{3,2,1,0:T(8,128)} %multiply_add_fusion.2), channel_id=1, source_target_pairs={{0,8},{8,16},{16,24},{24,32},{32,40},{40,48},{48,56},{56,64},{64,7... | collective-permute-start | bytes 688136 | tf_op jit(solution)/shard_map/while/body/eval_jaxpr/ppermute | solution.py:12
  634.7 215.0 %all-gather.5.cloned.1.call-start = ((), (), s32[]{:S(2)}) async-start(), calls=%async_computation.3 | async-start | bytes 15138816 | tf_op jit(solution)/shard_map/all_gather | solution.py:148
  749.7 13.1 %collective-permute-start.7 = (bf16[32,2,3584]{2,0,1:T(8,128)(2,1)S(1)}, bf16[32,2,3584]{2,0,1:T(8,128)(2,1)S(1)}, u32[]{:S(2)}, u32[]{:S(2)}) collective-permute-start(bf16[32,2,3584]{2,0,1:T(8,128)(2,1)S(1)} %collective-permute-done.6), channel_id=1, source_target_pairs={{0,7},{1,0},{2,1},{3,2},{4,3},{5,4},{6,5},{7,6},{8,15},{9,8},{10,9... | collective-permute-start | bytes 1376264 | tf_op jit(solution)/shard_map/ppermute | solution.py:140
  (28 other events, 2904.7 us)
Sparse Core Ops, SparseCore 0:
  10.6 94.5 all-gather.2
  634.9 83.3 reduce-scatter.1
  720.9 128.7 all-gather.4
